TPU v7x, 128 devices: a whole 4x4x4 slice. The times are simulated.
128 devices in a mesh: lon: 16 (over z, y_hi, core), lat: 8 (over x, y_lo).
Axes of the slice: x: 4, y: 4 (y_hi: 2, y_lo: 2; y = y_hi * 2 + y_lo), z: 4, core: 2. Of those that a mesh axis runs over, the one named last changes fastest.
Arguments:
- thermal_anomaly: float32 [16, 1024, 2048], P(None, 'lat', 'lon'), may hold values from -6 to 6
- saltiness_anomaly: float32 [16, 1024, 2048], P(None, 'lat', 'lon'), may hold values from -5 to 5
- zonal_transport_ratio: float32 [16, 1024, 2048], P(None, 'lat', 'lon'), may hold values from -0.4 to 0.4
- meridional_transport_ratio: float32 [16, 1024, 2048], P(None, 'lat', 'lon'), may hold values from -0.4 to 0.4
- water_indicator: int32 [16, 1024, 2048], P(None, 'lat', 'lon'), may hold values 0 or 1
- water_layer_tally: int32 [1024, 2048], P('lat', 'lon'), may hold values from 0 to 16
Outputs:
- advanced_thermal: float32 [16, 1024, 2048], P(None, 'lat', 'lon')
- advanced_saltiness: float32 [16, 1024, 2048], P(None, 'lat', 'lon')
All inputs are finite; a program needn't handle non-finite values. No bound on the sum of `water_indicator` on one device may be relied on, other than what follows from the above.
Results may differ from a plain program's by a relative error of at most 0.0003.
Values sent between devices are 32-bit elements; how exact they have to be, the bound alone decides.
A program may use at most 192 MiB of HBM per device.

v0:
```python
import functools

import jax
import jax.numpy as jnp
from jax import lax
from jax.experimental import pallas as pl
from jax.experimental.pallas import tpu as pltpu
from jax.sharding import PartitionSpec as P

MESH = pl.DeviceIdType.MESH
DIFFUSIVITY = 0.12
LIMIT_FLOOR = 0.01
BIG = 1e30

LEVELS = 16
TILE = 128
HALO = 3
ROWS = TILE + 2 * HALO
SPAN = 18
GROUPS = 7
RUN = 20
EDGE_ROWS = RUN + 2 * HALO
LAST = GROUPS - 1
TAIL = TILE - LAST * RUN

T, S, U, V, WET = range(5)
UP, LO, AX, AY, LOW, DX, DY = range(7)


def roll(value, shift):
    return pltpu.roll(value, shift % 128, 1)


def east(value):
    return roll(value, -1)


def west(value):
    return roll(value, 1)


def flux_row(f, x, base, count):
    wet = [f[WET, base - 1 + i] for i in range(count + 2)]
    tracers = [[f[q, base - 1 + i] for i in range(count + 2)] for q in (T, S)]
    previous = [None, None]
    for i in range(count + 1):
        row = base - 1 + i
        v_mask = wet[i] * wet[i + 1]
        half_y = 0.5 * f[V, row] * v_mask
        speed_y = jnp.abs(half_y)
        mix_y = DIFFUSIVITY * v_mask
        if i > 0:
            u_mask = wet[i] * east(wet[i])
            half_x = 0.5 * f[U, row] * u_mask
            speed_x = jnp.abs(half_x)
            mix_x = DIFFUSIVITY * u_mask
            sea = wet[i] > 0.0
        for n in range(2):
            q, north = tracers[n][i], tracers[n][i + 1]
            slope_y = north - q
            anti_y = speed_y * slope_y
            low_y = half_y * (north + q) - anti_y
            if i > 0:
                right = east(q)
                slope_x = right - q
                anti_x = speed_x * slope_x
                low_x = half_x * (right + q) - anti_x
                low = q - ((low_x - west(low_x)) + (low_y - previous[n]))
                x[UP, n, row] = jnp.where(sea, jnp.maximum(q, low), -BIG)
                x[LO, n, row] = jnp.where(sea, jnp.minimum(q, low), BIG)
                x[AX, n, row] = anti_x
                x[LOW, n, row] = low
                x[DX, n, row] = mix_x * slope_x
            x[AY, n, row] = anti_y
            x[DY, n, row] = mix_y * slope_y
            previous[n] = low_y


def ratio_row(x, r, base, count):
    for n in range(2):
        anti = x[AY, n, base - 1]
        below_in, below_out = jnp.maximum(anti, 0.0), jnp.minimum(anti, 0.0)
        upper = [x[UP, n, base - 1 + i] for i in range(count + 2)]
        lower = [x[LO, n, base - 1 + i] for i in range(count + 2)]
        for i in range(count):
            row = base + i
            high, least = upper[i + 1], lower[i + 1]
            q_max = jnp.maximum(
                jnp.maximum(jnp.maximum(east(high), west(high)), high),
                jnp.maximum(upper[i], upper[i + 2]),
            )
            q_min = jnp.minimum(
                jnp.minimum(jnp.minimum(east(least), west(least)), least),
                jnp.minimum(lower[i], lower[i + 2]),
            )
            anti_x = x[AX, n, row]
            anti_w = west(anti_x)
            anti_y = x[AY, n, row]
            above_in, above_out = jnp.maximum(anti_y, 0.0), jnp.minimum(anti_y, 0.0)
            inflow = (jnp.maximum(anti_w, 0.0) - jnp.minimum(anti_x, 0.0)) + (below_in - above_out)
            outflow = (jnp.maximum(anti_x, 0.0) - jnp.minimum(anti_w, 0.0)) + (above_in - below_out)
            low = x[LOW, n, row]
            r[0, n, row] = jnp.minimum(1.0, (q_max - low) / jnp.maximum(inflow, LIMIT_FLOOR))
            r[1, n, row] = jnp.minimum(1.0, (low - q_min) / jnp.maximum(outflow, LIMIT_FLOOR))
            below_in, below_out = above_in, above_out


def final_row(x, r, base, count, emit):
    for n in range(2):
        into = [r[0, n, base - 1 + i] for i in range(count + 2)]
        out = [r[1, n, base - 1 + i] for i in range(count + 2)]
        previous = None
        for i in range(count + 1):
            row = base - 1 + i
            anti_y = x[AY, n, row]
            limit_y = jnp.where(
                anti_y >= 0.0, jnp.minimum(into[i + 1], out[i]), jnp.minimum(into[i], out[i + 1])
            )
            flux_y = limit_y * anti_y - x[DY, n, row]
            if i > 0:
                anti_x = x[AX, n, row]
                limit_x = jnp.where(
                    anti_x >= 0.0,
                    jnp.minimum(east(into[i]), out[i]),
                    jnp.minimum(into[i], east(out[i])),
                )
                flux_x = limit_x * anti_x - x[DX, n, row]
                emit(n, i - 1, x[LOW, n, row] - ((flux_x - west(flux_x)) + (flux_y - previous)))
            previous = flux_y


def mirrored(value, lane):
    for bit in (64, 32, 16, 8, 4, 2, 1):
        if bit == 64:
            value = roll(value, 64)
        else:
            value = jnp.where(lax.rem(lane // bit, 2) == 1, roll(value, bit), roll(value, -bit))
    return value


def kernel(
    lons, lats,
    t_in, s_in, u_in, v_in, ind_in, tally_in, t_out, s_out,
    nat, nat_i, nat_t, f, x, r, e, xe, re, eq, own, late,
    to_east, to_west, from_west, from_east, late_east, late_west, late_from_west, late_from_east,
    result, in_sem, out_sem, send_sem, recv_sem,
):
    lon, lat = lax.axis_index("lon"), lax.axis_index("lat")
    top = lat // (lats - 1)
    is_top, has_south = lat == lats - 1, lat > 0
    right, left = lax.rem(lon + 1, lons), lax.rem(lon + lons - 1, lons)
    north_lon = lon + top * (lons - 1 - 2 * lon)
    north_lat = lat + 1 - top

    loads = [
        pltpu.make_async_copy(src, dst, in_sem.at[i])
        for i, (src, dst) in enumerate(
            [
                (ind_in, nat_i), (tally_in, nat_t), (t_in, nat.at[T]),
                (s_in, nat.at[S]), (u_in, nat.at[U]), (v_in, nat.at[V]),
            ]
        )
    ]
    for copy in loads:
        copy.start()

    barrier = pltpu.get_barrier_semaphore()

    def greet(at_lon, at_lat):
        pl.semaphore_signal(barrier, inc=1, device_id={"lon": at_lon, "lat": at_lat}, device_id_type=MESH)

    greet(right, lat)
    greet(left, lat)
    greet(north_lon, north_lat)

    @pl.when(has_south)
    def _():
        greet(lon, lat - 1)

    lane = lax.broadcasted_iota(jnp.int32, (LEVELS, 128), 1)
    level = lax.broadcasted_iota(jnp.int32, (LEVELS, 128), 0)
    group = lane // SPAN
    slot = lane - group * SPAN

    def window(value):
        return jnp.where(lane < 6, value, roll(value, 12))

    def placed(value, at, into):
        first = at * SPAN + HALO
        return jnp.where((lane >= first) & (lane < first + 12), roll(value, first), into)

    for copy in loads:
        copy.wait()

    @pl.when(lat == 0)
    def _():
        f[:, 0:HALO] = jnp.zeros((5, HALO, LEVELS, 128), jnp.float32)

    def pack(groups, row, carry):
        acc = [jnp.zeros((LEVELS, 128), jnp.float32) for _ in range(5)]
        for g in range(groups):
            j = g * RUN + row

            def strided(ref):
                return jnp.concatenate(
                    [ref[pl.ds(j, 8, stride=TILE), :], ref[pl.ds(j + 8 * TILE, 8, stride=TILE), :]], axis=0
                )

            values = [strided(nat.at[q]) for q in range(4)]
            tally = jnp.broadcast_to(nat_t[pl.ds(j, 1), :], (LEVELS, 128))
            values.append(jnp.where((strided(nat_i) == 1) & (level < tally), 1.0, 0.0).astype(jnp.float32))
            for q in range(5):
                f[q, j + HALO] = values[q]
                acc[q] = placed(window(values[q]), g, acc[q])
        for q in range(5):
            own[q, row] = acc[q]
        return carry

    lax.fori_loop(0, TAIL, functools.partial(pack, GROUPS), 0)
    lax.fori_loop(TAIL, RUN, functools.partial(pack, GROUPS - 1), 0)

    def columns(source, row, eastward, westward):
        over, under = jnp.zeros((LEVELS, 128), jnp.float32), jnp.zeros((LEVELS, 128), jnp.float32)
        for q in range(5):
            mine = (slot >= 3 * q) & (slot < 3 * q + 3)
            value = source[q, row]
            over = jnp.where(mine, roll(value, 3 * q - 12), over)
            under = jnp.where(mine, roll(value, 3 * q - 3), under)
        eastward[row] = over
        westward[row] = under

    def columns_loop(row, carry):
        columns(own, row, to_east, to_west)
        return carry

    lax.fori_loop(0, RUN, columns_loop, 0)

    @pl.when(has_south)
    def _():
        pl.semaphore_wait(barrier, 4)

    @pl.when(lat == 0)
    def _():
        pl.semaphore_wait(barrier, 3)

    def remote(src, dst, send, recv, at_lon, at_lat):
        return pltpu.make_async_remote_copy(
            src_ref=src, dst_ref=dst, send_sem=send_sem.at[send], recv_sem=recv_sem.at[recv],
            device_id={"lon": at_lon, "lat": at_lat}, device_id_type=MESH,
        )

    southern, northern = f.at[:, pl.ds(0, HALO)], f.at[:, pl.ds(TILE + HALO, HALO)]
    send_north = remote(
        f.at[:, pl.ds(TILE, HALO)], f.at[:, pl.ds(top * (TILE + HALO), HALO)], 0, top, north_lon, north_lat
    )
    send_south = remote(f.at[:, pl.ds(HALO, HALO)], northern, 1, 1, lon, lat - 1)
    from_south = remote(southern, southern, 0, 0, lon, lat)
    from_north = remote(northern, northern, 0, 1, lon, lat)
    send_east = remote(to_east, from_west, 2, 2, right, lat)
    send_west = remote(to_west, from_east, 3, 3, left, lat)
    send_late_east = remote(late_east, late_from_west, 4, 4, right, lat)
    send_late_west = remote(late_west, late_from_east, 5, 5, left, lat)

    send_north.start()

    @pl.when(has_south)
    def _():
        send_south.start()

    send_east.start()
    send_west.start()

    def flux_loop(i, carry):
        flux_row(f, x, 4 + 6 * i, 6)
        return carry

    lax.fori_loop(0, 21, flux_loop, 0)

    from_north.wait_recv()
    send_north.wait_send()

    @pl.when(has_south)
    def _():
        from_south.wait_recv()
        send_south.wait_send()

    @pl.when(is_top)
    def _():
        above = TILE + HALO
        for q in (T, S, WET, U):
            rows = [mirrored(f[q, above + i], lane) for i in (2, 1, 0)]
            for i in range(3):
                f[q, above + i] = -rows[i] if q == U else rows[i]
        rows = [mirrored(f[V, above + i], lane) for i in (2, 1, 0)]
        f[V, above - 1] = 0.5 * (f[V, above - 1] - rows[0])
        f[V, above] = -rows[1]
        f[V, above + 1] = -rows[2]

    for row in range(HALO):
        for q in range(5):
            ahead = TILE + HALO + row - (1 if q == V else 0)
            value = placed(window(f[q, row]), 0, jnp.zeros((LEVELS, 128), jnp.float32))
            late[q, row] = placed(window(f[q, ahead]), LAST, value)
        columns(late, row, late_east, late_west)
    send_late_east.start()
    send_late_west.start()

    @pl.when(is_top)
    def _():
        for i in range(3):
            f[U, TILE + HALO + i] = east(f[U, TILE + HALO + i])

    def flux_rest(i, carry):
        flux_row(f, x, 1 + 126 * i, 6)
        return carry

    lax.fori_loop(0, 2, flux_rest, 0)

    def ratio_loop(i, carry):
        ratio_row(x, r, 2 + 5 * i, 5)
        return carry

    lax.fori_loop(0, 26, ratio_loop, 0)

    send_east.wait()
    send_west.wait()
    send_late_east.wait()
    send_late_west.wait()

    def joined(source, q, row, west_part, east_part):
        value = jnp.where(slot < 3, roll(west_part[row], -3 * q), source[q, row])
        return jnp.where(slot >= 15, roll(east_part[row], 15 - 3 * q), value)

    def join_loop(row, carry):
        for q in range(5):
            e[q, row + HALO] = joined(own, q, row, from_west, from_east)
        return carry

    lax.fori_loop(0, RUN, join_loop, 0)

    for row in range(HALO):
        for q in range(5):
            value = joined(late, q, row, late_from_west, late_from_east)
            late[q, row] = value
            at = HALO + TAIL + row - (1 if q == V else 0)
            e[q, at] = jnp.where(group == LAST, value, e[q, at])

    @pl.when(is_top)
    def _():
        for row in range(HALO):
            at = HALO + TAIL + row
            e[U, at] = jnp.where(group == LAST, east(e[U, at]), e[U, at])

    for row in range(HALO):
        for q in range(5):
            e[q, row] = jnp.where(group == 0, late[q, row], roll(e[q, RUN + row], SPAN))
            e[q, RUN + HALO + row] = roll(e[q, HALO + row], -SPAN)

    def edge_flux(i, carry):
        flux_row(e, xe, 1 + 6 * i, 6)
        return carry

    lax.fori_loop(0, 4, edge_flux, 0)

    def edge_ratio(i, carry):
        ratio_row(xe, re, 2 + 2 * i, 2)
        return carry

    lax.fori_loop(0, 11, edge_ratio, 0)

    def edge_final(i, carry):
        def emit(n, k, value):
            eq[n, 4 * i + k] = value

        final_row(xe, re, HALO + 4 * i, 4, emit)
        return carry

    lax.fori_loop(0, 5, edge_final, 0)

    def final_loop(i, carry):
        g = i // 5
        shift_w = lax.rem(128 - HALO - g * SPAN + 128, 128)
        shift_e = lax.rem(113 - g * SPAN + 128, 128)

        def emit(n, k, value):
            j = 4 * i + k
            edge = eq[n, j - g * RUN]
            value = jnp.where(lane < 3, pltpu.roll(edge, shift_w, 1), value)
            value = jnp.where(lane >= 125, pltpu.roll(edge, shift_e, 1), value)
            result[n, pl.ds(j, 8, stride=TILE), :] = value[:8]
            result[n, pl.ds(j + 8 * TILE, 8, stride=TILE), :] = value[8:]

        final_row(x, r, HALO + 4 * i, 4, emit)
        return carry

    lax.fori_loop(0, 32, final_loop, 0)

    stores = [
        pltpu.make_async_copy(result.at[n], dst, out_sem.at[n]) for n, dst in enumerate((t_out, s_out))
    ]
    for copy in stores:
        copy.start()
    for copy in stores:
        copy.wait()


def solution(mesh):
    lons, lats = mesh.shape["lon"], mesh.shape["lat"]

    def step(t, s, u, v, ind, tally):
        flat = (LEVELS * TILE, TILE)
        vector = (LEVELS, 128)
        vmem = lambda *shape: pltpu.VMEM(shape, jnp.float32)
        outs = pl.pallas_call(
            functools.partial(kernel, lons, lats),
            out_shape=[jax.ShapeDtypeStruct(flat, jnp.float32)] * 2,
            in_specs=[pl.BlockSpec(memory_space=pl.ANY)] * 6,
            out_specs=[pl.BlockSpec(memory_space=pl.ANY)] * 2,
            scratch_shapes=[
                vmem(4, *flat),
                pltpu.VMEM(flat, jnp.int32),
                pltpu.VMEM((TILE, TILE), jnp.int32),
                vmem(5, ROWS, *vector),
                vmem(7, 2, ROWS, *vector),
                vmem(2, 2, ROWS, *vector),
                vmem(5, EDGE_ROWS, *vector),
                vmem(7, 2, EDGE_ROWS, *vector),
                vmem(2, 2, EDGE_ROWS, *vector),
                vmem(2, RUN, *vector),
                vmem(5, RUN, *vector),
                vmem(5, HALO, *vector),
                *[vmem(RUN, *vector)] * 4,
                *[vmem(HALO, *vector)] * 4,
                vmem(2, *flat),
                pltpu.SemaphoreType.DMA((6,)),
                pltpu.SemaphoreType.DMA((2,)),
                pltpu.SemaphoreType.DMA((6,)),
                pltpu.SemaphoreType.DMA((6,)),
            ],
            compiler_params=pltpu.CompilerParams(
                collective_id=0, has_side_effects=True, vmem_limit_bytes=60 * 1024 * 1024
            ),
        )(t.reshape(flat), s.reshape(flat), u.reshape(flat), v.reshape(flat), ind.reshape(flat), tally)
        return tuple(out.reshape(LEVELS, TILE, TILE) for out in outs)

    spec = P(None, "lat", "lon")
    return jax.shard_map(
        step,
        mesh=mesh,
        in_specs=(spec,) * 5 + (P("lat", "lon"),),
        out_specs=(spec, spec),
        check_vma=False,
    )
```

profile of v0, /device:TPU:15, one launch (start us, length us, event | category | flops | bytes accessed | tf_op | source)
XLA Modules:
  0.0 46.5 jit_solution(7856707453099286013)
XLA Ops:
  0.6 42.5 %shard_map.77 = (f32[2048,128]{1,0:T(8,128)}, f32[2048,128]{1,0:T(8,128)}) custom-call(f32[2048,128]{1,0:T(8,128)} %bitcast.9, f32[2048,128]{1,0:T(8,128)} %bitcast.10, f32[2048,128]{1,0:T(8,128)} %bitcast.11, f32[2048,128]{1,0:T(8,128)} %bitcast.12, s32[2048,128]{1,0:T(8,128)} %bitcast.13, s32[128,128]{1,0:T(8,128)} %tally_in.1), custom_call_target="tpu_custom_call" | custom-call | tf_op jit(solution)/shard_map/pallas_call | solution.py:414
  43.2 0.0 copy-start
  43.2 2.4 %copy.10 = f32[16,128,128]{2,1,0:T(8,128)} copy(f32[16,128,128]{2,1,0:T(8,128)} %bitcast.8) | data formatting | bytes 2097152
  45.6 0.0 copy-done
  45.6 1.0 %copy.11 = f32[16,128,128]{2,1,0:T(8,128)} copy(f32[16,128,128]{2,1,0:T(8,128)S(1)} %bitcast.7) | data formatting | bytes 2097152
Async XLA Ops:
  43.2 2.4 %copy-start = (f32[2048,128]{1,0:T(8,128)S(1)}, f32[2048,128]{1,0:T(8,128)}, u32[]{:S(2)}) copy-start(f32[2048,128]{1,0:T(8,128)} %get-tuple-element.5) | copy-start | bytes 3145732
where the time goes:
time: 46.7 us; the launch traced here: 46.5 us
  Pallas kernels  42.5 us (91%)
  local copies, waits for them, and re-layouts  3.36 us (7%)
  between operations  0.65 us (1%)
    pallas_call x1, Pallas kernels, step(): pl.pallas_call(functools.partial(kernel, lons, lats), out_shape=[jax.Shap...  42.5 us
    unnamed x4, local copies, waits for them, and re-layouts  3.36 us

commit v1 on v0

--- a/solution.py
+++ b/solution.py
@@ -21,6 +21,9 @@
 RUN = 20
 EDGE_ROWS = RUN + 2 * HALO
 LAST = GROUPS - 1
+FLUX_ROWS, RATIO_ROWS, FINAL_ROWS = 6, 5, 8
+EDGE_FLUX, EDGE_RATIO, EDGE_FINAL = 6, 11, 10
+PART = 32
 TAIL = TILE - LAST * RUN
 
 T, S, U, V, WET = range(5)
@@ -141,7 +144,7 @@
 def kernel(
     lons, lats,
     t_in, s_in, u_in, v_in, ind_in, tally_in, t_out, s_out,
-    nat, nat_i, nat_t, f, x, r, e, xe, re, eq, own, late,
+    nat_i, nat_t, f, x, r, e, xe, re, eq, own, late,
     to_east, to_west, from_west, from_east, late_east, late_west, late_from_west, late_from_east,
     result, in_sem, out_sem, send_sem, recv_sem,
 ):
@@ -152,17 +155,14 @@
     north_lon = lon + top * (lons - 1 - 2 * lon)
     north_lat = lat + 1 - top
 
-    loads = [
-        pltpu.make_async_copy(src, dst, in_sem.at[i])
-        for i, (src, dst) in enumerate(
-            [
-                (ind_in, nat_i), (tally_in, nat_t), (t_in, nat.at[T]),
-                (s_in, nat.at[S]), (u_in, nat.at[U]), (v_in, nat.at[V]),
-            ]
-        )
-    ]
-    for copy in loads:
-        copy.start()
+    tally_load = pltpu.make_async_copy(tally_in, nat_t, in_sem.at[5])
+    tally_load.start()
+
+    inputs = [(ind_in, nat_i), (t_in, f.at[T, pl.ds(HALO, TILE)]), (s_in, f.at[S, pl.ds(HALO, TILE)])]
+    inputs += [(u_in, f.at[U, pl.ds(HALO, TILE)]), (v_in, f.at[V, pl.ds(HALO, TILE)])]
+    for i, (src, dst) in enumerate(inputs):
+        for k in range(LEVELS):
+            pltpu.make_async_copy(src.at[k], dst.at[:, k], in_sem.at[i]).start()
 
     barrier = pltpu.get_barrier_semaphore()
 
@@ -182,58 +182,42 @@
     group = lane // SPAN
     slot = lane - group * SPAN
 
-    def window(value):
-        return jnp.where(lane < 6, value, roll(value, 12))
-
     def placed(value, at, into):
         first = at * SPAN + HALO
-        return jnp.where((lane >= first) & (lane < first + 12), roll(value, first), into)
-
-    for copy in loads:
-        copy.wait()
+        return jnp.where((lane >= first) & (lane < first + 12), roll(value, first + 6), into)
+
+    def split(fields, row, store, eastward, westward):
+        over, under = jnp.zeros((LEVELS, 128), jnp.float32), jnp.zeros((LEVELS, 128), jnp.float32)
+        for q in range(5):
+            store[q, row] = jnp.where(slot < 9, roll(fields[q], -6), roll(fields[q], 6))
+            mine = (slot >= 3 * q) & (slot < 3 * q + 3)
+            over = jnp.where(mine, roll(fields[q], 3 * q - 6), over)
+            under = jnp.where(mine, roll(fields[q], 3 * q - 9), under)
+        eastward[row] = over
+        westward[row] = under
 
     @pl.when(lat == 0)
     def _():
         f[:, 0:HALO] = jnp.zeros((5, HALO, LEVELS, 128), jnp.float32)
+
+    tally_load.wait()
+    for i, (_, dst) in enumerate(inputs):
+        pltpu.make_async_copy(dst, dst, in_sem.at[i]).wait()
 
     def pack(groups, row, carry):
         acc = [jnp.zeros((LEVELS, 128), jnp.float32) for _ in range(5)]
         for g in range(groups):
             j = g * RUN + row
-
-            def strided(ref):
-                return jnp.concatenate(
-                    [ref[pl.ds(j, 8, stride=TILE), :], ref[pl.ds(j + 8 * TILE, 8, stride=TILE), :]], axis=0
-                )
-
-            values = [strided(nat.at[q]) for q in range(4)]
             tally = jnp.broadcast_to(nat_t[pl.ds(j, 1), :], (LEVELS, 128))
-            values.append(jnp.where((strided(nat_i) == 1) & (level < tally), 1.0, 0.0).astype(jnp.float32))
+            wet = jnp.where((nat_i[j] == 1) & (level < tally), 1.0, 0.0).astype(jnp.float32)
+            f[WET, j + HALO] = wet
             for q in range(5):
-                f[q, j + HALO] = values[q]
-                acc[q] = placed(window(values[q]), g, acc[q])
-        for q in range(5):
-            own[q, row] = acc[q]
+                acc[q] = placed(wet if q == WET else f[q, j + HALO], g, acc[q])
+        split(acc, row, own, to_east, to_west)
         return carry
 
     lax.fori_loop(0, TAIL, functools.partial(pack, GROUPS), 0)
     lax.fori_loop(TAIL, RUN, functools.partial(pack, GROUPS - 1), 0)
-
-    def columns(source, row, eastward, westward):
-        over, under = jnp.zeros((LEVELS, 128), jnp.float32), jnp.zeros((LEVELS, 128), jnp.float32)
-        for q in range(5):
-            mine = (slot >= 3 * q) & (slot < 3 * q + 3)
-            value = source[q, row]
-            over = jnp.where(mine, roll(value, 3 * q - 12), over)
-            under = jnp.where(mine, roll(value, 3 * q - 3), under)
-        eastward[row] = over
-        westward[row] = under
-
-    def columns_loop(row, carry):
-        columns(own, row, to_east, to_west)
-        return carry
-
-    lax.fori_loop(0, RUN, columns_loop, 0)
 
     @pl.when(has_south)
     def _():
@@ -271,10 +255,10 @@
     send_west.start()
 
     def flux_loop(i, carry):
-        flux_row(f, x, 4 + 6 * i, 6)
-        return carry
-
-    lax.fori_loop(0, 21, flux_loop, 0)
+        flux_row(f, x, 4 + FLUX_ROWS * i, FLUX_ROWS)
+        return carry
+
+    lax.fori_loop(0, 126 // FLUX_ROWS, flux_loop, 0)
 
     from_north.wait_recv()
     send_north.wait_send()
@@ -297,11 +281,12 @@
         f[V, above + 1] = -rows[2]
 
     for row in range(HALO):
+        fields = []
         for q in range(5):
             ahead = TILE + HALO + row - (1 if q == V else 0)
-            value = placed(window(f[q, row]), 0, jnp.zeros((LEVELS, 128), jnp.float32))
-            late[q, row] = placed(window(f[q, ahead]), LAST, value)
-        columns(late, row, late_east, late_west)
+            value = placed(f[q, row], 0, jnp.zeros((LEVELS, 128), jnp.float32))
+            fields.append(placed(f[q, ahead], LAST, value))
+        split(fields, row, late, late_east, late_west)
     send_late_east.start()
     send_late_west.start()
 
@@ -311,16 +296,16 @@
             f[U, TILE + HALO + i] = east(f[U, TILE + HALO + i])
 
     def flux_rest(i, carry):
-        flux_row(f, x, 1 + 126 * i, 6)
+        flux_row(f, x, 1 + 129 * i, 3)
         return carry
 
     lax.fori_loop(0, 2, flux_rest, 0)
 
     def ratio_loop(i, carry):
-        ratio_row(x, r, 2 + 5 * i, 5)
-        return carry
-
-    lax.fori_loop(0, 26, ratio_loop, 0)
+        ratio_row(x, r, 2 + RATIO_ROWS * i, RATIO_ROWS)
+        return carry
+
+    lax.fori_loop(0, 130 // RATIO_ROWS, ratio_loop, 0)
 
     send_east.wait()
     send_west.wait()
@@ -357,68 +342,65 @@
             e[q, RUN + HALO + row] = roll(e[q, HALO + row], -SPAN)
 
     def edge_flux(i, carry):
-        flux_row(e, xe, 1 + 6 * i, 6)
-        return carry
-
-    lax.fori_loop(0, 4, edge_flux, 0)
+        flux_row(e, xe, 1 + EDGE_FLUX * i, EDGE_FLUX)
+        return carry
+
+    lax.fori_loop(0, 24 // EDGE_FLUX, edge_flux, 0)
 
     def edge_ratio(i, carry):
-        ratio_row(xe, re, 2 + 2 * i, 2)
-        return carry
-
-    lax.fori_loop(0, 11, edge_ratio, 0)
+        ratio_row(xe, re, 2 + EDGE_RATIO * i, EDGE_RATIO)
+        return carry
+
+    lax.fori_loop(0, 22 // EDGE_RATIO, edge_ratio, 0)
 
     def edge_final(i, carry):
         def emit(n, k, value):
-            eq[n, 4 * i + k] = value
-
-        final_row(xe, re, HALO + 4 * i, 4, emit)
-        return carry
-
-    lax.fori_loop(0, 5, edge_final, 0)
+            eq[n, EDGE_FINAL * i + k] = jnp.where(slot >= 15, roll(value, 12), value)
+
+        final_row(xe, re, HALO + EDGE_FINAL * i, EDGE_FINAL, emit)
+        return carry
+
+    lax.fori_loop(0, RUN // EDGE_FINAL, edge_final, 0)
+
+    border = (lane < 3) | (lane >= 125)
 
     def final_loop(i, carry):
-        g = i // 5
-        shift_w = lax.rem(128 - HALO - g * SPAN + 128, 128)
-        shift_e = lax.rem(113 - g * SPAN + 128, 128)
-
         def emit(n, k, value):
-            j = 4 * i + k
-            edge = eq[n, j - g * RUN]
-            value = jnp.where(lane < 3, pltpu.roll(edge, shift_w, 1), value)
-            value = jnp.where(lane >= 125, pltpu.roll(edge, shift_e, 1), value)
-            result[n, pl.ds(j, 8, stride=TILE), :] = value[:8]
-            result[n, pl.ds(j + 8 * TILE, 8, stride=TILE), :] = value[8:]
-
-        final_row(x, r, HALO + 4 * i, 4, emit)
-        return carry
-
-    lax.fori_loop(0, 32, final_loop, 0)
-
-    stores = [
-        pltpu.make_async_copy(result.at[n], dst, out_sem.at[n]) for n, dst in enumerate((t_out, s_out))
-    ]
-    for copy in stores:
-        copy.start()
-    for copy in stores:
-        copy.wait()
+            j = FINAL_ROWS * i + k
+            g = j // RUN
+            shift = lax.rem(113 - g * SPAN + 128, 128)
+            result[n, j] = jnp.where(border, pltpu.roll(eq[n, j - g * RUN], shift, 1), value)
+
+        final_row(x, r, HALO + FINAL_ROWS * i, FINAL_ROWS, emit)
+        return carry
+
+    def part_loop(i, carry):
+        lax.fori_loop(i * (PART // FINAL_ROWS), (i + 1) * (PART // FINAL_ROWS), final_loop, 0)
+        rows = pl.ds(pl.multiple_of(i * PART, PART), PART)
+        for n, dst in enumerate((t_out, s_out)):
+            for k in range(LEVELS):
+                pltpu.make_async_copy(result.at[n, rows, k], dst.at[k, rows], out_sem.at[n]).start()
+        return carry
+
+    lax.fori_loop(0, TILE // PART, part_loop, 0)
+    for n in range(2):
+        pltpu.make_async_copy(result.at[n], result.at[n], out_sem.at[n]).wait()
 
 
 def solution(mesh):
     lons, lats = mesh.shape["lon"], mesh.shape["lat"]
 
     def step(t, s, u, v, ind, tally):
-        flat = (LEVELS * TILE, TILE)
+        shape = (LEVELS, TILE, TILE)
         vector = (LEVELS, 128)
         vmem = lambda *shape: pltpu.VMEM(shape, jnp.float32)
         outs = pl.pallas_call(
             functools.partial(kernel, lons, lats),
-            out_shape=[jax.ShapeDtypeStruct(flat, jnp.float32)] * 2,
+            out_shape=[jax.ShapeDtypeStruct(shape, jnp.float32)] * 2,
             in_specs=[pl.BlockSpec(memory_space=pl.ANY)] * 6,
             out_specs=[pl.BlockSpec(memory_space=pl.ANY)] * 2,
             scratch_shapes=[
-                vmem(4, *flat),
-                pltpu.VMEM(flat, jnp.int32),
+                pltpu.VMEM((TILE, *vector), jnp.int32),
                 pltpu.VMEM((TILE, TILE), jnp.int32),
                 vmem(5, ROWS, *vector),
                 vmem(7, 2, ROWS, *vector),
@@ -431,7 +413,7 @@
                 vmem(5, HALO, *vector),
                 *[vmem(RUN, *vector)] * 4,
                 *[vmem(HALO, *vector)] * 4,
-                vmem(2, *flat),
+                vmem(2, TILE, *vector),
                 pltpu.SemaphoreType.DMA((6,)),
                 pltpu.SemaphoreType.DMA((2,)),
                 pltpu.SemaphoreType.DMA((6,)),
@@ -440,8 +422,8 @@
             compiler_params=pltpu.CompilerParams(
                 collective_id=0, has_side_effects=True, vmem_limit_bytes=60 * 1024 * 1024
             ),
-        )(t.reshape(flat), s.reshape(flat), u.reshape(flat), v.reshape(flat), ind.reshape(flat), tally)
-        return tuple(out.reshape(LEVELS, TILE, TILE) for out in outs)
+        )(t, s, u, v, ind, tally)
+        return tuple(outs)
 
     spec = P(None, "lat", "lon")
     return jax.shard_map(

time: 46.7 us -> 39.2 us (0.84)
  Pallas kernels: 42.5 us -> 34.9 us
    pallas_call x1, Pallas kernels: 42.5 us -> 34.9 us  [step(): pl.pallas_call(functools.partial(kernel, lons, lats), out_shape=[jax.Shap...]
where the time goes in v1:
time: 39.2 us; the launch traced here: 39 us
  Pallas kernels  34.9 us (89%)
  local copies, waits for them, and re-layouts  3.36 us (9%)
  between operations  0.65 us (2%)
    pallas_call x1, Pallas kernels, step(): pl.pallas_call(functools.partial(kernel, lons, lats), out_shape=[jax.Shap...  34.9 us
    unnamed x4, local copies, waits for them, and re-layouts  3.36 us

profile of v1, /device:TPU:15, one launch (start us, length us, event | category | flops | bytes accessed | tf_op | source)
XLA Modules:
  0.0 39.0 jit_solution(6237879670169702034)
XLA Ops:
  0.6 34.9 %shard_map.77 = (f32[16,128,128]{2,1,0:T(8,128)}, f32[16,128,128]{2,1,0:T(8,128)}) custom-call(f32[16,128,128]{2,1,0:T(8,128)} %t_in.1, f32[16,128,128]{2,1,0:T(8,128)} %s_in.1, f32[16,128,128]{2,1,0:T(8,128)} %u_in.1, f32[16,128,128]{2,1,0:T(8,128)} %v_in.1, s32[16,128,128]{2,1,0:T(8,128)} %ind_in.1, s32[128,128]{1,0:T(8,128)} %tally_in.1), custom_call_target="tpu_custom_call" | custom-call | tf_op jit(solution)/shard_map/pallas_call | solution.py:397
  35.6 0.0 copy-start
  35.6 2.4 %copy.10 = f32[16,128,128]{2,1,0:T(8,128)} copy(f32[16,128,128]{2,1,0:T(8,128)} %get-tuple-element.4) | data formatting | bytes 2097152
  38.0 0.0 copy-done
  38.0 1.0 %copy.11 = f32[16,128,128]{2,1,0:T(8,128)} copy(f32[16,128,128]{2,1,0:T(8,128)S(1)} %copy-done) | data formatting | bytes 2097152
Async XLA Ops:
  35.6 2.4 %copy-start = (f32[16,128,128]{2,1,0:T(8,128)S(1)}, f32[16,128,128]{2,1,0:T(8,128)}, u32[]{:S(2)}) copy-start(f32[16,128,128]{2,1,0:T(8,128)} %get-tuple-element.5) | copy-start | bytes 3145732

commit v2 on v1

--- a/solution.py
+++ b/solution.py
@@ -21,7 +21,7 @@
 RUN = 20
 EDGE_ROWS = RUN + 2 * HALO
 LAST = GROUPS - 1
-FLUX_ROWS, RATIO_ROWS, FINAL_ROWS = 6, 5, 8
+FLUX_ROWS, RATIO_ROWS, FINAL_ROWS = 6, 6, 8
 EDGE_FLUX, EDGE_RATIO, EDGE_FINAL = 6, 11, 10
 PART = 32
 TAIL = TILE - LAST * RUN
@@ -143,7 +143,7 @@
 
 def kernel(
     lons, lats,
-    t_in, s_in, u_in, v_in, ind_in, tally_in, t_out, s_out,
+    t_in, s_in, u_in, v_in, ind_in, tally_in, t_out, s_out, e_out,
     nat_i, nat_t, f, x, r, e, xe, re, eq, own, late,
     to_east, to_west, from_west, from_east, late_east, late_west, late_from_west, late_from_east,
     result, in_sem, out_sem, send_sem, recv_sem,
@@ -155,14 +155,30 @@
     north_lon = lon + top * (lons - 1 - 2 * lon)
     north_lat = lat + 1 - top
 
-    tally_load = pltpu.make_async_copy(tally_in, nat_t, in_sem.at[5])
+    fields = [(t_in, f.at[T, pl.ds(HALO, TILE)]), (s_in, f.at[S, pl.ds(HALO, TILE)])]
+    fields += [(u_in, f.at[U, pl.ds(HALO, TILE)]), (v_in, f.at[V, pl.ds(HALO, TILE)]), (ind_in, nat_i)]
+
+    def load_rows(first, last, sem):
+        for q, (src, dst) in enumerate(fields):
+            for j in range(first, last):
+                pltpu.make_async_copy(src.at[:, j], dst.at[j], in_sem.at[sem + (q == WET)]).start()
+
+    def await_rows(first, last, sem):
+        rows = f.at[pl.ds(0, WET), pl.ds(first + HALO, last - first)]
+        pltpu.make_async_copy(rows, rows, in_sem.at[sem]).wait()
+        rows = nat_i.at[pl.ds(first, last - first)]
+        pltpu.make_async_copy(rows, rows, in_sem.at[sem + 1]).wait()
+
+    tally_load = pltpu.make_async_copy(tally_in, nat_t, in_sem.at[6])
     tally_load.start()
-
-    inputs = [(ind_in, nat_i), (t_in, f.at[T, pl.ds(HALO, TILE)]), (s_in, f.at[S, pl.ds(HALO, TILE)])]
-    inputs += [(u_in, f.at[U, pl.ds(HALO, TILE)]), (v_in, f.at[V, pl.ds(HALO, TILE)])]
-    for i, (src, dst) in enumerate(inputs):
+    load_rows(0, HALO, 0)
+    load_rows(TILE - HALO, TILE, 2)
+    load_rows(HALO, 8, 4)
+    load_rows(TILE - 8, TILE - HALO, 4)
+    for q, (src, dst) in enumerate(fields):
         for k in range(LEVELS):
-            pltpu.make_async_copy(src.at[k], dst.at[:, k], in_sem.at[i]).start()
+            inner = pl.ds(8, TILE - 16)
+            pltpu.make_async_copy(src.at[k, inner], dst.at[inner, k], in_sem.at[4 + (q == WET)]).start()
 
     barrier = pltpu.get_barrier_semaphore()
 
@@ -200,24 +216,15 @@
     def _():
         f[:, 0:HALO] = jnp.zeros((5, HALO, LEVELS, 128), jnp.float32)
 
+    def sea_row(j):
+        tally = jnp.broadcast_to(nat_t[pl.ds(j, 1), :], (LEVELS, 128))
+        return jnp.where((nat_i[j] == 1) & (level < tally), 1.0, 0.0).astype(jnp.float32)
+
     tally_load.wait()
-    for i, (_, dst) in enumerate(inputs):
-        pltpu.make_async_copy(dst, dst, in_sem.at[i]).wait()
-
-    def pack(groups, row, carry):
-        acc = [jnp.zeros((LEVELS, 128), jnp.float32) for _ in range(5)]
-        for g in range(groups):
-            j = g * RUN + row
-            tally = jnp.broadcast_to(nat_t[pl.ds(j, 1), :], (LEVELS, 128))
-            wet = jnp.where((nat_i[j] == 1) & (level < tally), 1.0, 0.0).astype(jnp.float32)
-            f[WET, j + HALO] = wet
-            for q in range(5):
-                acc[q] = placed(wet if q == WET else f[q, j + HALO], g, acc[q])
-        split(acc, row, own, to_east, to_west)
-        return carry
-
-    lax.fori_loop(0, TAIL, functools.partial(pack, GROUPS), 0)
-    lax.fori_loop(TAIL, RUN, functools.partial(pack, GROUPS - 1), 0)
+    await_rows(0, HALO, 0)
+    await_rows(TILE - HALO, TILE, 2)
+    for j in (*range(HALO), *range(TILE - HALO, TILE)):
+        f[WET, j + HALO] = sea_row(j)
 
     @pl.when(has_south)
     def _():
@@ -251,6 +258,28 @@
     def _():
         send_south.start()
 
+    await_rows(HALO, TILE - HALO, 4)
+
+    def pack(groups, kept, row, carry):
+        acc = [jnp.zeros((LEVELS, 128), jnp.float32) for _ in range(5)]
+        for g in range(groups):
+            j = g * RUN + row
+            wet = sea_row(j)
+            if g != kept:
+                f[WET, j + HALO] = wet
+            for q in range(5):
+                acc[q] = placed(wet if q == WET else f[q, j + HALO], g, acc[q])
+        split(acc, row, own, to_east, to_west)
+        return carry
+
+    for first, last, groups, kept in (
+        (0, HALO, GROUPS, 0),
+        (HALO, TAIL - HALO, GROUPS, None),
+        (TAIL - HALO, TAIL, GROUPS, LAST),
+        (TAIL, RUN, LAST, None),
+    ):
+        lax.fori_loop(first, last, functools.partial(pack, groups, kept), 0)
+
     send_east.start()
     send_west.start()
 
@@ -259,6 +288,13 @@
         return carry
 
     lax.fori_loop(0, 126 // FLUX_ROWS, flux_loop, 0)
+
+    def ratio_loop(i, carry):
+        ratio_row(x, r, 5 + RATIO_ROWS * i, RATIO_ROWS)
+        return carry
+
+    lax.fori_loop(0, 120 // RATIO_ROWS, ratio_loop, 0)
+    ratio_row(x, r, 125, 4)
 
     from_north.wait_recv()
     send_north.wait_send()
@@ -295,23 +331,48 @@
         for i in range(3):
             f[U, TILE + HALO + i] = east(f[U, TILE + HALO + i])
 
+    def emit_at(base, n, k, value):
+        result[n, base - HALO + k] = value
+
+    def final_loop(i, carry):
+        base = 6 + FINAL_ROWS * i
+        final_row(x, r, base, FINAL_ROWS, functools.partial(emit_at, base))
+        return carry
+
+    lax.fori_loop(0, 120 // FINAL_ROWS, final_loop, 0)
+
+    def put(n, first, last):
+        rows = pl.ds(first, last - first)
+        return pltpu.make_async_copy(result.at[n, rows], (t_out, s_out)[n].at[rows], out_sem.at[n])
+
+    for n in range(2):
+        put(n, 8, 123).start()
+
     def flux_rest(i, carry):
         flux_row(f, x, 1 + 129 * i, 3)
         return carry
 
     lax.fori_loop(0, 2, flux_rest, 0)
 
-    def ratio_loop(i, carry):
-        ratio_row(x, r, 2 + RATIO_ROWS * i, RATIO_ROWS)
-        return carry
-
-    lax.fori_loop(0, 130 // RATIO_ROWS, ratio_loop, 0)
+    def ratio_rest(i, carry):
+        ratio_row(x, r, 2 + 127 * i, 3)
+        return carry
+
+    lax.fori_loop(0, 2, ratio_rest, 0)
+
+    def final_rest(i, carry):
+        base = HALO + 123 * i
+        final_row(x, r, base, 5, functools.partial(emit_at, base))
+        return carry
+
+    lax.fori_loop(0, 2, final_rest, 0)
+
+    for n in range(2):
+        put(n, 0, 8).start()
+        put(n, 123, TILE).start()
 
     send_east.wait()
     send_west.wait()
-    send_late_east.wait()
-    send_late_west.wait()
-
     def joined(source, q, row, west_part, east_part):
         value = jnp.where(slot < 3, roll(west_part[row], -3 * q), source[q, row])
         return jnp.where(slot >= 15, roll(east_part[row], 15 - 3 * q), value)
@@ -323,6 +384,8 @@
 
     lax.fori_loop(0, RUN, join_loop, 0)
 
+    send_late_east.wait()
+    send_late_west.wait()
     for row in range(HALO):
         for q in range(5):
             value = joined(late, q, row, late_from_west, late_from_east)
@@ -362,27 +425,46 @@
 
     lax.fori_loop(0, RUN // EDGE_FINAL, edge_final, 0)
 
+    put_edges = pltpu.make_async_copy(eq, e_out, out_sem.at[2])
+    put_edges.start()
+    for n in range(2):
+        rows = result.at[n]
+        pltpu.make_async_copy(rows, rows, out_sem.at[n]).wait()
+    put_edges.wait()
+
+
+def finish(t_in, s_in, e_in, t_out, s_out, eq, result, in_sem, out_sem):
+    edges = pltpu.make_async_copy(e_in, eq, in_sem.at[0])
+    edges.start()
+
+    def load(n, part):
+        rows = pl.ds(part * PART, PART)
+        return pltpu.make_async_copy((t_in, s_in)[n].at[rows], result.at[n, rows], in_sem.at[1 + n * (TILE // PART) + part])
+
+    for part in range(TILE // PART):
+        for n in range(2):
+            load(n, part).start()
+    lane = lax.broadcasted_iota(jnp.int32, (LEVELS, 128), 1)
     border = (lane < 3) | (lane >= 125)
 
-    def final_loop(i, carry):
-        def emit(n, k, value):
-            j = FINAL_ROWS * i + k
-            g = j // RUN
-            shift = lax.rem(113 - g * SPAN + 128, 128)
-            result[n, j] = jnp.where(border, pltpu.roll(eq[n, j - g * RUN], shift, 1), value)
-
-        final_row(x, r, HALO + FINAL_ROWS * i, FINAL_ROWS, emit)
-        return carry
-
-    def part_loop(i, carry):
-        lax.fori_loop(i * (PART // FINAL_ROWS), (i + 1) * (PART // FINAL_ROWS), final_loop, 0)
-        rows = pl.ds(pl.multiple_of(i * PART, PART), PART)
+    def patch(i, carry):
+        for n in range(2):
+            for k in range(FINAL_ROWS):
+                j = FINAL_ROWS * i + k
+                g = j // RUN
+                shift = lax.rem(113 - g * SPAN + 128, 128)
+                result[n, j] = jnp.where(border, pltpu.roll(eq[n, j - g * RUN], shift, 1), result[n, j])
+        return carry
+
+    edges.wait()
+    for part in range(TILE // PART):
+        for n in range(2):
+            load(n, part).wait()
+        lax.fori_loop(part * (PART // FINAL_ROWS), (part + 1) * (PART // FINAL_ROWS), patch, 0)
+        rows = pl.ds(part * PART, PART)
         for n, dst in enumerate((t_out, s_out)):
             for k in range(LEVELS):
                 pltpu.make_async_copy(result.at[n, rows, k], dst.at[k, rows], out_sem.at[n]).start()
-        return carry
-
-    lax.fori_loop(0, TILE // PART, part_loop, 0)
     for n in range(2):
         pltpu.make_async_copy(result.at[n], result.at[n], out_sem.at[n]).wait()
 
@@ -396,9 +478,10 @@
         vmem = lambda *shape: pltpu.VMEM(shape, jnp.float32)
         outs = pl.pallas_call(
             functools.partial(kernel, lons, lats),
-            out_shape=[jax.ShapeDtypeStruct(shape, jnp.float32)] * 2,
+            out_shape=[jax.ShapeDtypeStruct((TILE, *vector), jnp.float32)] * 2
+            + [jax.ShapeDtypeStruct((2, RUN, *vector), jnp.float32)],
             in_specs=[pl.BlockSpec(memory_space=pl.ANY)] * 6,
-            out_specs=[pl.BlockSpec(memory_space=pl.ANY)] * 2,
+            out_specs=[pl.BlockSpec(memory_space=pl.ANY)] * 3,
             scratch_shapes=[
                 pltpu.VMEM((TILE, *vector), jnp.int32),
                 pltpu.VMEM((TILE, TILE), jnp.int32),
@@ -414,8 +497,8 @@
                 *[vmem(RUN, *vector)] * 4,
                 *[vmem(HALO, *vector)] * 4,
                 vmem(2, TILE, *vector),
-                pltpu.SemaphoreType.DMA((6,)),
-                pltpu.SemaphoreType.DMA((2,)),
+                pltpu.SemaphoreType.DMA((7,)),
+                pltpu.SemaphoreType.DMA((3,)),
                 pltpu.SemaphoreType.DMA((6,)),
                 pltpu.SemaphoreType.DMA((6,)),
             ],
@@ -423,7 +506,21 @@
                 collective_id=0, has_side_effects=True, vmem_limit_bytes=60 * 1024 * 1024
             ),
         )(t, s, u, v, ind, tally)
-        return tuple(outs)
+        return tuple(
+            pl.pallas_call(
+                finish,
+                out_shape=[jax.ShapeDtypeStruct(shape, jnp.float32)] * 2,
+                in_specs=[pl.BlockSpec(memory_space=pl.ANY)] * 3,
+                out_specs=[pl.BlockSpec(memory_space=pl.ANY)] * 2,
+                scratch_shapes=[
+                    vmem(2, RUN, *vector),
+                    vmem(2, TILE, *vector),
+                    pltpu.SemaphoreType.DMA((1 + 2 * TILE // PART,)),
+                    pltpu.SemaphoreType.DMA((2,)),
+                ],
+                compiler_params=pltpu.CompilerParams(vmem_limit_bytes=60 * 1024 * 1024),
+            )(*outs)
+        )
 
     spec = P(None, "lat", "lon")
     return jax.shard_map(

time: 39.2 us -> 34.1 us (0.87)
  local copies, waits for them, and re-layouts: 3.36 us -> 0 us
  Pallas kernels: 34.9 us -> 33.4 us
    pallas_call x1, Pallas kernels: 34.9 us -> 28.9 us  [step(): pl.pallas_call(functools.partial(kernel, lons, lats), out_shape=[jax.Shap...]
    pallas_call x0 -> x1, Pallas kernels: none -> 4.45 us  [step(): pl.pallas_call(finish, out_shape=[jax.ShapeDtypeStruct(shape, jnp.float32...]
    unnamed x4 -> x0, local copies, waits for them, and re-layouts: 3.36 us -> none
where the time goes in v2:
time: 34.1 us; the launch traced here: 34 us
  Pallas kernels  33.4 us (98%)
  between operations  0.64 us (2%)
    pallas_call x1, Pallas kernels, step(): pl.pallas_call(functools.partial(kernel, lons, lats), out_shape=[jax.Shap...  28.9 us
    pallas_call x1, Pallas kernels, step(): pl.pallas_call(finish, out_shape=[jax.ShapeDtypeStruct(shape, jnp.float32...  4.45 us

profile of v2, /device:TPU:15, one launch (start us, length us, event | category | flops | bytes accessed | tf_op | source)
XLA Modules:
  0.0 34.0 jit_solution(17846234256256789403)
XLA Ops:
  0.6 28.9 %shard_map.77 = (f32[128,16,128]{2,1,0:T(8,128)}, f32[128,16,128]{2,1,0:T(8,128)}, f32[2,20,16,128]{3,2,1,0:T(8,128)}) custom-call(f32[16,128,128]{2,1,0:T(8,128)} %t_in.1, f32[16,128,128]{2,1,0:T(8,128)} %s_in.1, f32[16,128,128]{2,1,0:T(8,128)} %u_in.1, f32[16,128,128]{2,1,0:T(8,128)} %v_in.1, s32[16,128,128]{2,1,0:T(8,128)} %ind_in.1, s32[128,128]{1,0:T(8,128)} %tally_in.1), custom_call_target="tpu_custom_call" | custom-call | tf_op jit(solution)/shard_map/pallas_call | solution.py:479
  29.6 4.5 %shard_map.78 = (f32[16,128,128]{2,1,0:T(8,128)}, f32[16,128,128]{2,1,0:T(8,128)}) custom-call(f32[128,16,128]{2,1,0:T(8,128)} %get-tuple-element.5.t_in, f32[128,16,128]{2,1,0:T(8,128)} %get-tuple-element.6.s_in, f32[2,20,16,128]{3,2,1,0:T(8,128)} %get-tuple-element.7.e_in), custom_call_target="tpu_custom_call" | custom-call | tf_op jit(solution)/shard_map/pallas_call | solution.py:510
